TPU v7x, 512 devices: a whole 4x8x8 slice. The times are simulated.
512 devices in a mesh: fib: 64 (over z, x, core), pln: 8 (over y).
Axes of the slice: x: 4, y: 8, z: 8, core: 2. Of those that a mesh axis runs over, the one named last changes fastest.
Arguments:
- nodal_values: float32 [8, 64, 288, 1000], P('pln', 'fib'), may hold values from -6 to 6
- interp_matrix: float32 [1000, 512], replicated, may hold values from -0.1875 to 0.1875
- count_table: int32 [8, 64, 3], P('pln'), may hold values from 1 to 96, as said below
- slot_order: int32 [8, 64, 192], P('pln', 'fib'), may hold values from 0 to 191, each once within a row
- start_basis: float32 [768, 128], replicated, may hold values from -6 to 6
Outputs:
- core_values: float32 [8, 64, 128, 128], P('pln', 'fib')
Inputs may be any that keep to these rules, and one draw needn't show every extreme that they name: count_table[j, o, d] elements of owner o come from the source d places before it along fib, cyclically; for every owner the 3 entries sum to 192 and one equals 96. `slot_order`: each owner's row is a permutation.
All inputs are finite; a program needn't handle non-finite values.
Results may differ from a plain program's by a relative error of at most 0.0003.
Values sent between devices are 32-bit elements; how exact they have to be, the bound alone decides.
A program may use at most 64 MiB of HBM per device.

v0:
```python
import jax
import jax.numpy as jnp
from jax import lax
from jax.sharding import PartitionSpec as P

NX = 768
TILES_DEV = 1


def shifted(value, axis, by):
    peers = lax.axis_size(axis)
    return lax.ppermute(value, axis, [(i, (i + by) % peers) for i in range(peers)])


def per_device(nodal_values, interp_matrix, count_table, slot_order, start_basis):
    full_precision = lax.Precision.HIGHEST
    node_rows = nodal_values[0, 0]
    owner_table = count_table[0]
    brick_order = slot_order[0, 0]
    owners = lax.axis_size("fib")
    own_index = lax.axis_index("fib")
    window = owner_table.shape[1]
    capacity = node_rows.shape[0] // window
    elements = brick_order.shape[0]
    tiles_total = TILES_DEV * owners
    block_width = NX // owners
    send_start = []
    running = jnp.int32(0)
    for distance in range(window):
        send_start.append(running)
        column = owner_table[:, distance]
        running = running + lax.dynamic_index_in_dim(
            column, (own_index + distance) % owners, 0, keepdims=False
        )
    own_counts = lax.dynamic_index_in_dim(owner_table, own_index, 0, keepdims=False)
    positions = jnp.arange(elements, dtype=jnp.int32)
    combined_index = jnp.zeros((elements,), jnp.int32)
    offset = jnp.int32(0)
    for distance in range(window - 1, -1, -1):
        taken_count = own_counts[distance]
        inside = (positions >= offset) & (positions < offset + taken_count)
        combined_index = jnp.where(inside, distance * capacity + positions - offset, combined_index)
        offset = offset + taken_count
    brick_source = jnp.zeros((elements,), jnp.int32).at[brick_order].set(combined_index)
    grid_rows = jnp.dot(
        node_rows, interp_matrix, precision=full_precision, preferred_element_type=jnp.float32
    )
    received = []
    for distance in range(window):
        send_piece = lax.dynamic_slice_in_dim(grid_rows, send_start[distance], capacity, 0)
        if distance > 0:
            send_piece = shifted(send_piece, "fib", distance)
        received.append(send_piece)
    brick_values = jnp.concatenate(received, axis=0)[brick_source]
    brick_grid = brick_values.reshape(tiles_total, block_width, brick_values.shape[1] // 4)
    fibre_field = lax.all_to_all(brick_grid, "fib", split_axis=0, concat_axis=1, tiled=True)
    gram_part = jnp.einsum("txf,tyf->xy", fibre_field, fibre_field, precision=full_precision)
    gram_matrix = lax.psum(gram_part, ("fib", "pln"))
    image_matrix = jnp.dot(gram_matrix, start_basis, precision=full_precision)
    normal_matrix = jnp.dot(image_matrix.T, image_matrix, precision=full_precision)
    lower_factor = jnp.linalg.cholesky(normal_matrix)
    new_basis = jax.scipy.linalg.solve_triangular(lower_factor, image_matrix.T, lower=True).T
    core_values = jnp.einsum("xk,txf->tkf", new_basis, fibre_field, precision=full_precision)
    return core_values[None]


def solution(mesh):
    placed = (P("pln", "fib", None, None), P(), P("pln", None, None), P("pln", "fib", None), P())
    return jax.shard_map(
        per_device,
        mesh=mesh,
        in_specs=placed,
        out_specs=P("pln", "fib", None, None),
        check_vma=False,
    )
```

profile of v0, /device:TPU:1, one launch (start us, length us, event | category | flops | bytes accessed | tf_op | source)
XLA Modules:
  0.0 377.5 jit_solution(10091446328949841219)
XLA Ops:
  6.5 0.0 copy-start
  6.5 0.0 all-reduce.2.cloned.1.call-start
  6.5 0.8 copy.12
  7.4 0.7 constant_dynamic-slice_fusion.4
  11.2 0.0 copy-done
  11.2 0.0 copy-start.2
  11.2 0.0 copy-start.3
  11.2 3.4 fusion
  14.7 0.1 fusion.8
  14.7 3.9 %collective-permute-start.1 = (f32[96,512]{1,0:T(8,128)S(1)}, f32[96,512]{1,0:T(8,128)S(1)}, u32[]{:S(2)}, u32[]{:S(2)}) collective-permute-start(f32[96,512]{1,0:T(8,128)S(1)} %get-tuple-element.6), channel_id=1, source_target_pairs={{0,16},{8,24},{16,32},{24,40},{32,48},{40,56},{48,64},{56,72},{64,... | collective-permute-start | bytes 589832 | tf_op jit(solution)/shard_map/ppermute | solution.py:12
  18.7 4.0 %collective-permute-start = (f32[96,512]{1,0:T(8,128)S(1)}, f32[96,512]{1,0:T(8,128)S(1)}, u32[]{:S(2)}, u32[]{:S(2)}) collective-permute-start(f32[96,512]{1,0:T(8,128)S(1)} %get-tuple-element.7), channel_id=1, source_target_pairs={{0,8},{8,16},{16,24},{24,32},{32,40},{40,48},{48,56},{56,64},{64,7... | collective-permute-start | bytes 589832 | tf_op jit(solution)/shard_map/ppermute | solution.py:12
  22.6 0.0 copy-done.2
  22.6 0.7 constant_dynamic-slice_fusion.2
  25.2 0.6 and_select_fusion.1
  25.8 0.0 copy-done.3
  25.8 1.2 scatter_custom_fusion
  27.1 5.9 %collective-permute-done.1 = f32[96,512]{1,0:T(8,128)S(1)} collective-permute-done((f32[96,512]{1,0:T(8,128)S(1)}, f32[96,512]{1,0:T(8,128)S(1)}, u32[]{:S(2)}, u32[]{:S(2)}) %collective-permute-start.1) | collective-permute-done | bytes 196640 | tf_op jit(solution)/shard_map/ppermute | solution.py:12
  33.0 0.0 collective-permute-done
  33.0 0.9 gather_fusion
  33.9 0.1 reshape.65
  34.0 25.5 %all_to_all.4 = f32[64,12,128]{2,1,0:T(8,128)S(1)} all-to-all(f32[64,12,128]{2,1,0:T(8,128)S(1)} %reshape.65), channel_id=1, replica_groups=mesh['fib'=64,'pln'=8] {'fib'}, dimensions={0} | all-to-all | bytes 786432 | tf_op jit(solution)/shard_map/all_to_all | solution.py:56
  59.6 0.0 copy-start.1
  59.6 3.4 fusion.10
  63.0 0.0 all-reduce.2.cloned.1.call-update
  63.0 278.1 %all-reduce.2.cloned.1.call-done = f32[768,768]{1,0:T(8,128)} async-done(((f32[768,768]{1,0:T(8,128)}), f32[768,768]{1,0:T(8,128)}) %all-reduce.2.cloned.1.call-update) | async-done | bytes 2359312 | tf_op jit(solution)/shard_map/psum | solution.py:58
  341.1 0.0 copy-done.1
  341.1 3.7 fusion.11
  344.8 0.8 fusion.12
  345.6 0.1 copy.8
  345.7 11.7 %cholesky.16 = f32[128,128]{1,0:T(8,128)S(1)} custom-call(f32[128,128]{1,0:T(8,128)S(1)} %fusion.5), custom_call_target="Cholesky" | custom-call | tf_op jit(solution)/shard_map/jit(cholesky)/cholesky | solution.py:61
  357.4 0.6 compare_reduce_fusion
  358.1 0.7 fusion.2
  358.8 9.8 %custom-call.7 = f32[1,128,128]{1,2,0:T(8,128)S(1)} custom-call(f32[1,128,128]{2,1,0:T(8,128)S(1)} %fusion.2), custom_call_target="InvertDiagBlocksLowerTriangular" | custom-call | tf_op jit(solution)/shard_map/jit(_solve_triangular)/triangular_solve | solution.py:62
  368.6 0.5 fusion.3
  369.1 0.8 convolution_bitcast_fusion
  369.9 0.7 copy.9
  (8 shorter events, 0.1 us)
Async XLA Ops:
  6.5 4.7 %copy-start = (f32[1000,512]{1,0:T(8,128)S(1)}, f32[1000,512]{1,0:T(8,128)}, u32[]{:S(2)}) copy-start(f32[1000,512]{1,0:T(8,128)} %param.6) | copy-start | bytes 6144004
  6.5 334.6 %all-reduce.2.cloned.1.call-start = ((), (), s32[]{:S(2)}) async-start(), calls=%async_computation.1 | async-start | bytes 4718592 | tf_op jit(solution)/shard_map/psum | solution.py:58
  11.2 11.4 %copy-start.2 = (s32[1,64,3]{1,0,2:T(1,128)S(1)}, s32[1,64,3]{1,0,2:T(1,128)}, u32[]{:S(2)}) copy-start(s32[1,64,3]{1,0,2:T(1,128)} %param.7) | copy-start | bytes 2308
  11.2 14.6 %copy-start.3 = (s32[1,1,192]{2,1,0:T(1,128)S(1)}, s32[1,1,192]{2,1,0:T(1,128)}, u32[]{:S(2)}) copy-start(s32[1,1,192]{2,1,0:T(1,128)} %param.8) | copy-start | bytes 2308
  14.7 18.3 %collective-permute-start.1 = (f32[96,512]{1,0:T(8,128)S(1)}, f32[96,512]{1,0:T(8,128)S(1)}, u32[]{:S(2)}, u32[]{:S(2)}) collective-permute-start(f32[96,512]{1,0:T(8,128)S(1)} %get-tuple-element.6), channel_id=1, source_target_pairs={{0,16},{8,24},{16,32},{24,40},{32,48},{40,56},{48,64},{56,72},{64,... | collective-permute-start | bytes 589832 | tf_op jit(solution)/shard_map/ppermute | solution.py:12
  18.7 14.3 %collective-permute-start = (f32[96,512]{1,0:T(8,128)S(1)}, f32[96,512]{1,0:T(8,128)S(1)}, u32[]{:S(2)}, u32[]{:S(2)}) collective-permute-start(f32[96,512]{1,0:T(8,128)S(1)} %get-tuple-element.7), channel_id=1, source_target_pairs={{0,8},{8,16},{16,24},{24,32},{32,40},{40,48},{48,56},{56,64},{64,7... | collective-permute-start | bytes 589832 | tf_op jit(solution)/shard_map/ppermute | solution.py:12
  59.6 281.6 %copy-start.1 = (f32[768,128]{1,0:T(8,128)S(1)}, f32[768,128]{1,0:T(8,128)}, u32[]{:S(2)}) copy-start(f32[768,128]{1,0:T(8,128)} %param.9) | copy-start | bytes 1179652
Sparse Core Ops, SparseCore 0:
  63.1 277.9 all-reduce.1
where the time goes:
time: 378 us; the launch traced here: 377 us
  waiting for transfers between devices  284 us (75%)
  blocking collectives  25.5 us (7%)
  other arithmetic  23.5 us (6%)
  between operations  18.7 us (5%)
  matrix products  12.6 us (3%)
  starting transfers between devices  7.9 us (2%)
  local copies, waits for them, and re-layouts  5.23 us (1%)
    psum x1, waiting for transfers between devices, per_device(): gram_matrix = lax.psum(gram_part, ('fib', 'pln'))  278 us
    all_to_all x1, blocking collectives, per_device(): lax.all_to_all(brick_grid, 'fib', split_axis=0, concat_axis=1, tiled=True)  25.5 us
    another operation x3, other arithmetic, per_device(): lower_factor = jnp.linalg.cholesky(normal_matrix)  12.4 us
    another operation x2, other arithmetic, per_device(): jax.scipy.linalg.solve_triangular(lower_factor, image_matrix.T, lower=True)  10.5 us
    ppermute x2, starting transfers between devices, shifted(): lax.ppermute(value, axis, [(i, (i + by) % peers) for i in range(peers)])  7.89 us
  transfers between devices with their start and end apart: 3, of which 2 were waited for; matrix products, arithmetic and copies ran while one was open for 1% of the time, Pallas kernels for 0%

commit v1 on v0

--- a/solution.py
+++ b/solution.py
@@ -55,7 +55,8 @@
     brick_grid = brick_values.reshape(tiles_total, block_width, brick_values.shape[1] // 4)
     fibre_field = lax.all_to_all(brick_grid, "fib", split_axis=0, concat_axis=1, tiled=True)
     gram_part = jnp.einsum("txf,tyf->xy", fibre_field, fibre_field, precision=full_precision)
-    gram_matrix = lax.psum(gram_part, ("fib", "pln"))
+    partial = lax.psum(gram_part, "fib")
+    gram_matrix = lax.psum(partial, "pln")
     image_matrix = jnp.dot(gram_matrix, start_basis, precision=full_precision)
     normal_matrix = jnp.dot(image_matrix.T, image_matrix, precision=full_precision)
     lower_factor = jnp.linalg.cholesky(normal_matrix)

time: 378 us -> 387 us (1.024)
  waiting for transfers between devices: 284 us -> 291 us
    psum x1 -> x2, waiting for transfers between devices: 278 us -> 285 us  [the longest x1 197 us: per_device(): partial = lax.psum(gram_part, 'fib')]
  transfers between devices with their start and end apart: 3 -> 4, of which waited for: 2 -> 3; matrix products, arithmetic and copies ran while one was open for 1% -> 1% of each run, Pallas kernels for 0% -> 0%
where the time goes in v1:
time: 387 us; the launch traced here: 384 us
  waiting for transfers between devices  291 us (75%)
  blocking collectives  25.5 us (7%)
  other arithmetic  23.5 us (6%)
  between operations  18.7 us (5%)
  matrix products  12.6 us (3%)
  starting transfers between devices  8.12 us (2%)
  local copies, waits for them, and re-layouts  5.23 us (1%)
    psum x1, waiting for transfers between devices, per_device(): partial = lax.psum(gram_part, 'fib')  197 us
    psum x1, waiting for transfers between devices, per_device(): gram_matrix = lax.psum(partial, 'pln')  87.6 us
    all_to_all x1, blocking collectives, per_device(): lax.all_to_all(brick_grid, 'fib', split_axis=0, concat_axis=1, tiled=True)  25.5 us
    another operation x3, other arithmetic, per_device(): lower_factor = jnp.linalg.cholesky(normal_matrix)  12.4 us
    another operation x2, other arithmetic, per_device(): jax.scipy.linalg.solve_triangular(lower_factor, image_matrix.T, lower=True)  10.5 us
    ppermute x2, starting transfers between devices, shifted(): lax.ppermute(value, axis, [(i, (i + by) % peers) for i in range(peers)])  7.89 us
  transfers between devices with their start and end apart: 4, of which 3 were waited for; matrix products, arithmetic and copies ran while one was open for 1% of the time, Pallas kernels for 0%

profile of v1, /device:TPU:1, one launch (start us, length us, event | category | flops | bytes accessed | tf_op | source)
XLA Modules:
  0.0 384.3 jit_solution(14774030590271459519)
XLA Ops:
  6.5 0.0 copy-start
  6.5 0.0 all-reduce.3.cloned.1.call-start
  6.5 0.8 copy.12
  7.4 0.7 constant_dynamic-slice_fusion.4
  11.2 0.0 copy-done
  11.2 0.0 copy-start.2
  11.2 0.0 copy-start.3
  11.2 3.4 fusion
  14.7 0.1 fusion.8
  14.7 3.9 %collective-permute-start.1 = (f32[96,512]{1,0:T(8,128)S(1)}, f32[96,512]{1,0:T(8,128)S(1)}, u32[]{:S(2)}, u32[]{:S(2)}) collective-permute-start(f32[96,512]{1,0:T(8,128)S(1)} %get-tuple-element.6), channel_id=1, source_target_pairs={{0,16},{8,24},{16,32},{24,40},{32,48},{40,56},{48,64},{56,72},{64,... | collective-permute-start | bytes 589832 | tf_op jit(solution)/shard_map/ppermute | solution.py:12
  18.7 4.0 %collective-permute-start = (f32[96,512]{1,0:T(8,128)S(1)}, f32[96,512]{1,0:T(8,128)S(1)}, u32[]{:S(2)}, u32[]{:S(2)}) collective-permute-start(f32[96,512]{1,0:T(8,128)S(1)} %get-tuple-element.7), channel_id=1, source_target_pairs={{0,8},{8,16},{16,24},{24,32},{32,40},{40,48},{48,56},{56,64},{64,7... | collective-permute-start | bytes 589832 | tf_op jit(solution)/shard_map/ppermute | solution.py:12
  22.6 0.0 copy-done.2
  22.6 0.7 constant_dynamic-slice_fusion.2
  25.2 0.6 and_select_fusion.1
  25.8 0.0 copy-done.3
  25.8 1.2 scatter_custom_fusion
  27.1 5.9 %collective-permute-done.1 = f32[96,512]{1,0:T(8,128)S(1)} collective-permute-done((f32[96,512]{1,0:T(8,128)S(1)}, f32[96,512]{1,0:T(8,128)S(1)}, u32[]{:S(2)}, u32[]{:S(2)}) %collective-permute-start.1) | collective-permute-done | bytes 196640 | tf_op jit(solution)/shard_map/ppermute | solution.py:12
  33.0 0.0 collective-permute-done
  33.0 0.9 gather_fusion
  33.9 0.1 reshape.65
  34.0 25.5 %all_to_all.4 = f32[64,12,128]{2,1,0:T(8,128)S(1)} all-to-all(f32[64,12,128]{2,1,0:T(8,128)S(1)} %reshape.65), channel_id=1, replica_groups=mesh['fib'=64,'pln'=8] {'fib'}, dimensions={0} | all-to-all | bytes 786432 | tf_op jit(solution)/shard_map/all_to_all | solution.py:56
  59.6 3.4 fusion.10
  63.0 0.0 copy-start.1
  63.0 0.0 all-reduce.3.cloned.1.call-update
  63.0 0.2 all-reduce.5.cloned.1.call-start
  63.2 197.0 %all-reduce.3.cloned.1.call-done = f32[768,768]{1,0:T(8,128)} async-done(((f32[768,768]{1,0:T(8,128)}), f32[768,768]{1,0:T(8,128)}) %all-reduce.3.cloned.1.call-update) | async-done | bytes 2359312 | tf_op jit(solution)/shard_map/psum | solution.py:58
  260.3 0.0 all-reduce.5.cloned.1.call-update
  260.3 87.6 %all-reduce.5.cloned.1.call-done = f32[768,768]{1,0:T(8,128)} async-done(((f32[768,768]{1,0:T(8,128)}), f32[768,768]{1,0:T(8,128)}) %all-reduce.5.cloned.1.call-update) | async-done | bytes 2359312 | tf_op jit(solution)/shard_map/psum | solution.py:59
  347.9 0.0 copy-done.1
  347.9 3.7 fusion.11
  351.6 0.8 fusion.12
  352.4 0.1 copy.8
  352.5 11.7 %cholesky.16 = f32[128,128]{1,0:T(8,128)S(1)} custom-call(f32[128,128]{1,0:T(8,128)S(1)} %fusion.5), custom_call_target="Cholesky" | custom-call | tf_op jit(solution)/shard_map/jit(cholesky)/cholesky | solution.py:62
  364.2 0.6 compare_reduce_fusion
  364.9 0.7 fusion.2
  365.5 9.8 %custom-call.7 = f32[1,128,128]{1,2,0:T(8,128)S(1)} custom-call(f32[1,128,128]{2,1,0:T(8,128)S(1)} %fusion.2), custom_call_target="InvertDiagBlocksLowerTriangular" | custom-call | tf_op jit(solution)/shard_map/jit(_solve_triangular)/triangular_solve | solution.py:63
  375.4 0.5 fusion.3
  375.9 0.8 convolution_bitcast_fusion
  376.7 0.7 copy.9
  (8 shorter events, 0.1 us)
Async XLA Ops:
  6.5 4.7 %copy-start = (f32[1000,512]{1,0:T(8,128)S(1)}, f32[1000,512]{1,0:T(8,128)}, u32[]{:S(2)}) copy-start(f32[1000,512]{1,0:T(8,128)} %param.6) | copy-start | bytes 6144004
  6.5 253.7 %all-reduce.3.cloned.1.call-start = ((), (), s32[]{:S(2)}) async-start(), calls=%async_computation.1 | async-start | bytes 4718592 | tf_op jit(solution)/shard_map/psum | solution.py:58
  11.2 11.4 %copy-start.2 = (s32[1,64,3]{1,0,2:T(1,128)S(1)}, s32[1,64,3]{1,0,2:T(1,128)}, u32[]{:S(2)}) copy-start(s32[1,64,3]{1,0,2:T(1,128)} %param.7) | copy-start | bytes 2308
  11.2 14.6 %copy-start.3 = (s32[1,1,192]{2,1,0:T(1,128)S(1)}, s32[1,1,192]{2,1,0:T(1,128)}, u32[]{:S(2)}) copy-start(s32[1,1,192]{2,1,0:T(1,128)} %param.8) | copy-start | bytes 2308
  14.7 18.3 %collective-permute-start.1 = (f32[96,512]{1,0:T(8,128)S(1)}, f32[96,512]{1,0:T(8,128)S(1)}, u32[]{:S(2)}, u32[]{:S(2)}) collective-permute-start(f32[96,512]{1,0:T(8,128)S(1)} %get-tuple-element.6), channel_id=1, source_target_pairs={{0,16},{8,24},{16,32},{24,40},{32,48},{40,56},{48,64},{56,72},{64,... | collective-permute-start | bytes 589832 | tf_op jit(solution)/shard_map/ppermute | solution.py:12
  18.7 14.3 %collective-permute-start = (f32[96,512]{1,0:T(8,128)S(1)}, f32[96,512]{1,0:T(8,128)S(1)}, u32[]{:S(2)}, u32[]{:S(2)}) collective-permute-start(f32[96,512]{1,0:T(8,128)S(1)} %get-tuple-element.7), channel_id=1, source_target_pairs={{0,8},{8,16},{16,24},{24,32},{32,40},{40,48},{48,56},{56,64},{64,7... | collective-permute-start | bytes 589832 | tf_op jit(solution)/shard_map/ppermute | solution.py:12
  63.0 284.9 %copy-start.1 = (f32[768,128]{1,0:T(8,128)S(1)}, f32[768,128]{1,0:T(8,128)}, u32[]{:S(2)}) copy-start(f32[768,128]{1,0:T(8,128)} %param.9) | copy-start | bytes 1179652
  63.0 284.9 %all-reduce.5.cloned.1.call-start = ((), (), s32[]{:S(2)}) async-start(), calls=%async_computation.2 | async-start | bytes 4718592 | tf_op jit(solution)/shard_map/psum | solution.py:59
Sparse Core Ops, SparseCore 0:
  63.1 197.0 all-reduce.2
  262.6 85.2 all-reduce.4
